TPU v7x, 32 devices: a whole 2x2x4 slice. The times are simulated.
32 devices in a mesh: src: 8 (over y, x, core), dst: 4 (over z).
Axes of the slice: x: 2, y: 2, z: 4, core: 2. Of those that a mesh axis runs over, the one named last changes fastest.
Arguments:
- raw: bfloat16 [4096, 256], P(('src', 'dst')), may hold values from -6 to 6
- enc_w1: bfloat16 [256, 512], replicated, may hold values from -0.375 to 0.375
- enc_w2: bfloat16 [512, 256], replicated, may hold values from -0.25 to 0.25
- block_weights: float32 [512, 128, 128], P(('src', 'dst')), may hold values from -0.125 to 0.125
- block_cols: int32 [512], P(('src', 'dst')), may hold values from 0 to 3, as said below
- noise: bfloat16 [3, 4096, 256], P(None, ('src', 'dst')), may hold values from -3 to 3
Outputs:
- encoded: bfloat16 [4096, 256], P(('src', 'dst'))
- hops: bfloat16 [3, 4096, 256], P(None, ('src', 'dst'))
Inputs may be any that keep to these rules, and one draw needn't show every extreme that they name: `block_cols`: entry b of each device's 16 entries belongs to row block b // 2; row blocks 2j and 2j+1 of a device together name every column block exactly once, each naming 4 // 2 distinct ones.
All inputs are finite; a program needn't handle non-finite values.
Results may differ from a plain program's by a relative error of at most 0.0058.
Values may be sent and summed in bfloat16 or wider, within the bound.
A program may use at most 128 MiB of HBM per device.

v0:
```python
import jax
import jax.numpy as jnp
from jax import lax
from jax.sharding import PartitionSpec as P

HOPS = 3


def normalize_rows(z):
    return (z * lax.rsqrt(jnp.mean(z * z, axis=-1, keepdims=True) + 1e-06)).astype(jnp.bfloat16)


def shards(raw, enc_w1, enc_w2, block_weights, block_cols, noise):
    hidden = jax.nn.silu(jnp.dot(raw, enc_w1, preferred_element_type=jnp.float32)).astype(
        jnp.bfloat16
    )
    encoded = normalize_rows(jnp.dot(hidden, enc_w2, preferred_element_type=jnp.float32))
    own_rows = raw.shape[0]
    block_side = block_weights.shape[1]
    width = encoded.shape[1]
    feats = encoded
    kept = []
    for step in range(HOPS):
        group = lax.all_gather(feats, "dst", axis=0, tiled=True)
        col_count = group.shape[0] // block_side
        half = col_count // 2
        col_blocks = group.astype(jnp.float32).reshape(col_count, block_side, width)
        fetched = jnp.take(col_blocks, block_cols, axis=0)
        prods = jnp.einsum("bij,bjw->biw", block_weights, fetched, precision=lax.Precision.HIGHEST)
        mine = lax.psum_scatter(
            prods.reshape(own_rows * lax.axis_size("src") // block_side, half, block_side, width)
            .sum(axis=1)
            .reshape(own_rows * lax.axis_size("src"), width),
            "src",
            scatter_dimension=0,
            tiled=True,
        )
        feats = normalize_rows(mine + noise[step].astype(jnp.float32))
        kept.append(feats)
    return (encoded, jnp.stack(kept))


def solution(mesh):
    placed = (
        P(("src", "dst"), None),
        P(),
        P(),
        P(("src", "dst"), None, None),
        P(("src", "dst")),
        P(None, ("src", "dst"), None),
    )
    return jax.shard_map(
        shards,
        mesh=mesh,
        in_specs=placed,
        out_specs=(P(("src", "dst"), None), P(None, ("src", "dst"), None)),
        check_vma=False,
    )
```

profile of v0, /device:TPU:0, one launch (start us, length us, event | category | flops | bytes accessed | tf_op | source)
XLA Modules:
  0.0 204.7 jit_solution(9608763618662152512)
XLA Ops:
  7.2 0.0 copy-start
  7.2 0.0 reduce-scatter.4.cloned.1.call-start
  7.2 0.7 compare_and_fusion
  8.0 0.7 compare_select_fusion
  8.6 1.5 multiply_reduce_fusion.3
  10.1 0.1 multiply_convert_fusion.4
  10.2 0.0 copy-start.2
  10.2 15.7 %all_gather.9 = bf16[512,256]{1,0:T(8,128)(2,1)S(1)} all-gather(bf16[128,256]{1,0:T(8,128)(2,1)S(1)} %multiply_convert_fusion.4), channel_id=1, replica_groups=mesh['src'=8,'dst'=4] {'dst'}, dimensions={0}, use_global_device_ids=true | all-gather | bytes 327680 | tf_op jit(solution)/shard_map/all_gather | solution.py:24
  25.9 2.0 gather_fusion
  28.0 0.0 copy-done.2
  28.0 0.0 copy-done
  28.0 5.4 %bitcast_reduce_fusion.2 = f32[8,128,256]{1,2,0:T(8,128)S(1)} fusion(f32[16,128,128]{2,1,0:T(8,128)S(1)} %copy-done, f32[16,128,256]{2,1,0:T(8,128)} %gather_fusion, pred[16]{0:T(512)(128)(4,1)S(1)} %compare_and_fusion), kind=kOutput, calls=%fused_computation.5 | convolution fusion | flops 806092800 | bytes 4194320 | tf_op jit(solution)/shard_map/bij,bjw->biw/dot_general | solution.py:29
  33.4 0.0 copy-start.1
  33.4 1.3 copy.15
  34.8 0.0 reduce-scatter.4.cloned.1.call-update
  34.8 0.0 reduce-scatter.6.cloned.1.call-start
  34.9 37.6 %reduce-scatter.4.cloned.1.call-done = f32[128,256]{1,0:T(8,128)} async-done(((f32[1024,256]{1,0:T(8,128)}), f32[128,256]{1,0:T(8,128)}) %reduce-scatter.4.cloned.1.call-update) | async-done | bytes 131088 | tf_op jit(solution)/shard_map/reduce_scatter | solution.py:30
  72.4 0.0 copy-done.1
  72.4 1.0 multiply_reduce_fusion.2
  73.5 1.0 multiply_convert_fusion.3
  74.5 13.8 %all_gather.10 = bf16[512,256]{1,0:T(8,128)(2,1)S(1)} all-gather(bf16[128,256]{1,0:T(8,128)(2,1)S(1)} %multiply_convert_fusion.3), channel_id=1, replica_groups=mesh['src'=8,'dst'=4] {'dst'}, dimensions={0}, use_global_device_ids=true | all-gather | bytes 327680 | tf_op jit(solution)/shard_map/all_gather | solution.py:24
  88.3 2.0 gather_fusion.1
  90.4 5.4 %bitcast_reduce_fusion.1 = f32[8,128,256]{1,2,0:T(8,128)S(1)} fusion(f32[16,128,128]{2,1,0:T(8,128)S(1)} %copy-done, f32[16,128,256]{2,1,0:T(8,128)} %gather_fusion.1, pred[16]{0:T(512)(128)(4,1)S(1)} %compare_and_fusion), kind=kOutput, calls=%fused_computation.4 | convolution fusion | flops 806092800 | bytes 4194320 | tf_op jit(solution)/shard_map/bij,bjw->biw/dot_general | solution.py:29
  95.8 1.3 copy.17
  97.2 0.0 reduce-scatter.6.cloned.1.call-update
  97.2 0.0 reduce-scatter.8.cloned.1.call-start
  97.2 36.7 %reduce-scatter.6.cloned.1.call-done = f32[128,256]{1,0:T(8,128)} async-done(((f32[1024,256]{1,0:T(8,128)}), f32[128,256]{1,0:T(8,128)}) %reduce-scatter.6.cloned.1.call-update) | async-done | bytes 131088 | tf_op jit(solution)/shard_map/reduce_scatter | solution.py:30
  133.9 1.0 multiply_reduce_fusion.1
  134.9 1.0 multiply_convert_fusion.2
  135.9 14.1 %all_gather.11 = bf16[512,256]{1,0:T(8,128)(2,1)S(1)} all-gather(bf16[128,256]{1,0:T(8,128)(2,1)S(1)} %multiply_convert_fusion.2), channel_id=1, replica_groups=mesh['src'=8,'dst'=4] {'dst'}, dimensions={0}, use_global_device_ids=true | all-gather | bytes 327680 | tf_op jit(solution)/shard_map/all_gather | solution.py:24
  150.0 2.0 gather_fusion.2
  152.1 5.4 %bitcast_reduce_fusion = f32[8,128,256]{1,2,0:T(8,128)S(1)} fusion(f32[16,128,128]{2,1,0:T(8,128)S(1)} %copy-done, f32[16,128,256]{2,1,0:T(8,128)} %gather_fusion.2, pred[16]{0:T(512)(128)(4,1)S(1)} %compare_and_fusion), kind=kOutput, calls=%fused_computation.3 | convolution fusion | flops 806092800 | bytes 4194320 | tf_op jit(solution)/shard_map/bij,bjw->biw/dot_general | solution.py:29
  157.5 1.3 copy.19
  158.8 0.0 reduce-scatter.8.cloned.1.call-update
  158.9 36.6 %reduce-scatter.8.cloned.1.call-done = f32[128,256]{1,0:T(8,128)} async-done(((f32[1024,256]{1,0:T(8,128)}), f32[128,256]{1,0:T(8,128)}) %reduce-scatter.8.cloned.1.call-update) | async-done | bytes 131088 | tf_op jit(solution)/shard_map/reduce_scatter | solution.py:30
  195.5 1.0 multiply_reduce_fusion
  196.5 1.0 fusion.19
  197.5 0.7 pad_maximum_fusion
  (8 shorter events, 0.1 us)
Async XLA Ops:
  7.2 20.8 %copy-start = (f32[16,128,128]{2,1,0:T(8,128)S(1)}, f32[16,128,128]{2,1,0:T(8,128)}, u32[]{:S(2)}) copy-start(f32[16,128,128]{2,1,0:T(8,128)} %param.11) | copy-start | bytes 3145732
  7.2 65.3 %reduce-scatter.4.cloned.1.call-start = ((), (), s32[]{:S(2)}) async-start(), calls=%async_computation.3 | async-start | bytes 1179648 | tf_op jit(solution)/shard_map/reduce_scatter | solution.py:30
  10.2 17.7 %copy-start.2 = (bf16[128,256]{1,0:T(8,128)(2,1)}, bf16[128,256]{1,0:T(8,128)(2,1)S(1)}, u32[]{:S(2)}) copy-start(bf16[128,256]{1,0:T(8,128)(2,1)S(1)} %multiply_convert_fusion.4) | copy-start | bytes 196612
  33.4 39.0 %copy-start.1 = (bf16[3,128,256]{2,1,0:T(8,128)(2,1)S(1)}, bf16[3,128,256]{2,1,0:T(8,128)(2,1)}, u32[]{:S(2)}) copy-start(bf16[3,128,256]{2,1,0:T(8,128)(2,1)} %param.13) | copy-start | bytes 589828
  34.8 99.1 %reduce-scatter.6.cloned.1.call-start = ((), (), s32[]{:S(2)}) async-start(), calls=%async_computation.4 | async-start | bytes 1179648 | tf_op jit(solution)/shard_map/reduce_scatter | solution.py:30
  97.2 98.3 %reduce-scatter.8.cloned.1.call-start = ((), (), s32[]{:S(2)}) async-start(), calls=%async_computation.5 | async-start | bytes 1179648 | tf_op jit(solution)/shard_map/reduce_scatter | solution.py:30
Sparse Core Ops, SparseCore 0:
  34.9 37.4 reduce-scatter.3
  97.3 36.5 reduce-scatter.5
  159.0 36.4 reduce-scatter.7
where the time goes:
time: 205 us
  waiting for transfers between devices  111 us (54%)
  blocking collectives  43.6 us (21%)
  matrix products  17.8 us (9%)
  between operations  13.9 us (7%)
  local copies, waits for them, and re-layouts  10.1 us (5%)
  other arithmetic  8.34 us (4%)
    reduce_scatter x3, waiting for transfers between devices, shards(): lax.psum_scatter(prods.reshape(own_rows * lax.axis_size('src') // block_s...  111 us
    all_gather x3, blocking collectives, shards(): group = lax.all_gather(feats, 'dst', axis=0, tiled=True)  43.6 us
    dot_general x3, matrix products, shards(): jnp.einsum('bij,bjw->biw', block_weights, fetched, precision=lax.Precisio...  16.3 us
    gather x3, local copies, waits for them, and re-layouts, shards(): fetched = jnp.take(col_blocks, block_cols, axis=0)  6.1 us
  transfers between devices with their start and end apart: 3, of which 3 were waited for; matrix products, arithmetic and copies ran while one was open for 0% of the time, Pallas kernels for 0%

commit v1 on v0

--- a/solution.py
+++ b/solution.py
@@ -2,8 +2,38 @@
 import jax.numpy as jnp
 from jax import lax
 from jax.sharding import PartitionSpec as P
+from jax.lax import axis_index, axis_size, ppermute
 
 HOPS = 3
+
+
+def ticks_write(my_tile, ndim_at):
+    part_now = axis_index("dst")
+    plain = axis_size("dst")
+    pile = []
+    reached, long_array, passed = (plain, part_now, my_tile.shape[ndim_at])
+    for d, ii in enumerate(my_tile.shape):
+        pile.append(ii * reached if d == ndim_at else ii)
+    outer = jnp.zeros(pile, my_tile.dtype)
+    clean = a_next = my_tile
+    front = lax.dynamic_update_slice_in_dim(outer, my_tile, long_array * passed, axis=ndim_at)
+    for nth in range(1, reached // 2 + 1):
+        seen = []
+        for d in range(reached):
+            seen.append((d, (d + 1) % reached))
+        clean = ppermute(clean, axis_name="dst", perm=seen)
+        front = lax.dynamic_update_slice_in_dim(
+            front, clean, (long_array - nth) % reached * passed, axis=ndim_at
+        )
+        if 2 * nth < reached:
+            views = []
+            for d in range(reached):
+                views.append((d, (d - 1) % reached))
+            a_next = ppermute(a_next, axis_name="dst", perm=views)
+            front = lax.dynamic_update_slice_in_dim(
+                front, a_next, (long_array + nth) % reached * passed, axis=ndim_at
+            )
+    return front
 
 
 def normalize_rows(z):
@@ -21,7 +51,7 @@
     feats = encoded
     kept = []
     for step in range(HOPS):
-        group = lax.all_gather(feats, "dst", axis=0, tiled=True)
+        group = ticks_write(feats, 0)
         col_count = group.shape[0] // block_side
         half = col_count // 2
         col_blocks = group.astype(jnp.float32).reshape(col_count, block_side, width)

time: 205 us -> 190 us (0.927)
  blocking collectives: 43.6 us -> 0 us
  waiting for transfers between devices: 111 us -> 127 us
  starting transfers between devices: 0.12 us -> 13.1 us
    all_gather x3 -> x0, blocking collectives: 43.6 us -> none  [shards(): group = lax.all_gather(feats, 'dst', axis=0, tiled=True)]
    ppermute x0 -> x9, waiting for transfers between devices: none -> 25.9 us  [the longest x6 25.3 us: ticks_write(): clean = ppermute(clean, axis_name='dst', perm=seen)]
    ppermute x0 -> x9, starting transfers between devices: none -> 13 us  [the longest x3 6.78 us: ticks_write(): a_next = ppermute(a_next, axis_name='dst', perm=views)]
    reduce_scatter x3, waiting for transfers between devices: 111 us -> 101 us  [shards(): lax.psum_scatter(prods.reshape(own_rows * lax.axis_size('src') // block_s...]
    convert_element_type x3 -> x0, other arithmetic: 2.09 us -> none  [normalize_rows(): (z * lax.rsqrt(jnp.mean(z * z, axis=-1, keepdims=True) + 1e-06)).astype(j...]
    dynamic_update_slice x0 -> x3, other arithmetic: none -> 2.07 us  [ticks_write(): lax.dynamic_update_slice_in_dim(outer, my_tile, long_array * passed, axis...]
  transfers between devices with their start and end apart: 3 -> 12, of which waited for: 3 -> 10; matrix products, arithmetic and copies ran while one was open for 0% -> 0% of each run, Pallas kernels for 0% -> 0%
where the time goes in v1:
time: 190 us; the launch traced here: 189 us
  waiting for transfers between devices  127 us (67%)
  matrix products  17.9 us (9%)
  between operations  14 us (7%)
  starting transfers between devices  13.1 us (7%)
  local copies, waits for them, and re-layouts  10.3 us (5%)
  other arithmetic  6.94 us (4%)
    reduce_scatter x3, waiting for transfers between devices, shards(): lax.psum_scatter(prods.reshape(own_rows * lax.axis_size('src') // block_s...  101 us
    ppermute x6, waiting for transfers between devices, ticks_write(): clean = ppermute(clean, axis_name='dst', perm=seen)  25.3 us
    dot_general x3, matrix products, shards(): jnp.einsum('bij,bjw->biw', block_weights, fetched, precision=lax.Precisio...  16.3 us
    ppermute x3, starting transfers between devices, ticks_write(): a_next = ppermute(a_next, axis_name='dst', perm=views)  6.78 us
    ppermute x6, starting transfers between devices, ticks_write(): clean = ppermute(clean, axis_name='dst', perm=seen)  6.17 us
    gather x3, local copies, waits for them, and re-layouts, shards(): fetched = jnp.take(col_blocks, block_cols, axis=0)  6.1 us
    reduce_sum x3, local copies, waits for them, and re-layouts, shards(): mine = lax.psum_scatter(prods.reshape(own_rows * lax.axis_size('src') //...  3.98 us
  transfers between devices with their start and end apart: 12, of which 10 were waited for; matrix products, arithmetic and copies ran while one was open for 0% of the time, Pallas kernels for 0%

profile of v1, /device:TPU:0, one launch (start us, length us, event | category | flops | bytes accessed | tf_op | source)
XLA Modules:
  0.0 189.5 jit_solution(11668871444719183923)
XLA Ops:
  7.2 0.0 copy-start
  7.2 0.0 reduce-scatter.4.cloned.1.call-start
  7.2 1.6 multiply_reduce_fusion.3
  8.8 0.1 constant_dynamic-update-slice_fusion.11
  8.9 0.0 copy-start.2
  9.0 3.1 %collective-permute-start = (bf16[128,256]{1,0:T(8,128)(2,1)S(1)}, bf16[128,256]{1,0:T(8,128)(2,1)S(1)}, u32[]{:S(2)}, u32[]{:S(2)}) collective-permute-start(bf16[128,256]{1,0:T(8,128)(2,1)S(1)} %get-tuple-element.8), channel_id=1, source_target_pairs={{0,1},{1,2},{2,3},{3,0},{4,5},{5,6},{6,7},{7,4},{8,9},{9,10},{10,1... | collective-permute-start | bytes 196616 | tf_op jit(solution)/shard_map/ppermute | solution.py:24
  12.1 2.1 %collective-permute-start.1 = (bf16[128,256]{1,0:T(8,128)(2,1)S(1)}, bf16[128,256]{1,0:T(8,128)(2,1)S(1)}, u32[]{:S(2)}, u32[]{:S(2)}) collective-permute-start(bf16[128,256]{1,0:T(8,128)(2,1)S(1)} %get-tuple-element.8), channel_id=1, source_target_pairs={{0,3},{1,0},{2,1},{3,2},{4,7},{5,4},{6,5},{7,6},{8,11},{9,8},{10,9... | collective-permute-start | bytes 196616 | tf_op jit(solution)/shard_map/ppermute | solution.py:32
  14.2 2.2 %collective-permute-done = bf16[128,256]{1,0:T(8,128)(2,1)S(1)} collective-permute-done((bf16[128,256]{1,0:T(8,128)(2,1)S(1)}, bf16[128,256]{1,0:T(8,128)(2,1)S(1)}, u32[]{:S(2)}, u32[]{:S(2)}) %collective-permute-start) | collective-permute-done | bytes 65568 | tf_op jit(solution)/shard_map/ppermute | solution.py:24
  16.4 0.0 collective-permute-start.2
  16.4 0.6 collective-permute-done.1
  17.0 5.5 %collective-permute-done.2 = bf16[128,256]{1,0:T(8,128)(2,1)S(1)} collective-permute-done((bf16[128,256]{1,0:T(8,128)(2,1)S(1)}, bf16[128,256]{1,0:T(8,128)(2,1)S(1)}, u32[]{:S(2)}, u32[]{:S(2)}) %collective-permute-start.2) | collective-permute-done | bytes 65568 | tf_op jit(solution)/shard_map/ppermute | solution.py:24
  22.6 2.0 %gather_fusion = f32[16,128,256]{2,1,0:T(8,128)} fusion(f32[4,128,256]{2,1,0:T(8,128)S(1)} %convert.6, s32[1024]{0:T(1024)S(1)} %pad_clamp_fusion), kind=kCustom, calls=%fused_computation.clone | custom fusion | bytes 4194368 | tf_op jit(solution)/shard_map/jit(_take)/gather | solution.py:58
  24.6 5.4 %bitcast_reduce_fusion.2 = f32[8,128,256]{1,2,0:T(8,128)S(1)} fusion(f32[16,128,128]{2,1,0:T(8,128)S(1)} %copy-done, f32[16,128,256]{2,1,0:T(8,128)} %gather_fusion, pred[16]{0:T(512)(128)(4,1)S(1)} %compare_and_fusion), kind=kOutput, calls=%fused_computation.5 | convolution fusion | flops 806092800 | bytes 4194320 | tf_op jit(solution)/shard_map/bij,bjw->biw/dot_general | solution.py:59
  30.0 0.0 copy-start.1
  30.1 1.3 copy.15
  31.4 0.0 reduce-scatter.4.cloned.1.call-update
  31.4 0.0 reduce-scatter.6.cloned.1.call-start
  31.5 34.7 %reduce-scatter.4.cloned.1.call-done = f32[128,256]{1,0:T(8,128)} async-done(((f32[1024,256]{1,0:T(8,128)}), f32[128,256]{1,0:T(8,128)}) %reduce-scatter.4.cloned.1.call-update) | async-done | bytes 131088 | tf_op jit(solution)/shard_map/reduce_scatter | solution.py:60
  66.2 1.0 multiply_reduce_fusion.2
  67.2 1.0 constant_dynamic-update-slice_fusion.7
  68.2 1.5 collective-permute-start.3
  69.8 2.3 %collective-permute-start.4 = (bf16[128,256]{1,0:T(8,128)(2,1)S(1)}, bf16[128,256]{1,0:T(8,128)(2,1)S(1)}, u32[]{:S(2)}, u32[]{:S(2)}) collective-permute-start(bf16[128,256]{1,0:T(8,128)(2,1)S(1)} %get-tuple-element.6), channel_id=1, source_target_pairs={{0,3},{1,0},{2,1},{3,2},{4,7},{5,4},{6,5},{7,6},{8,11},{9,8},{10,9... | collective-permute-start | bytes 196616 | tf_op jit(solution)/shard_map/ppermute | solution.py:32
  72.1 2.8 %collective-permute-done.3 = bf16[128,256]{1,0:T(8,128)(2,1)S(1)} collective-permute-done((bf16[128,256]{1,0:T(8,128)(2,1)S(1)}, bf16[128,256]{1,0:T(8,128)(2,1)S(1)}, u32[]{:S(2)}, u32[]{:S(2)}) %collective-permute-start.3) | collective-permute-done | bytes 65568 | tf_op jit(solution)/shard_map/ppermute | solution.py:24
  74.9 0.0 collective-permute-start.5
  74.9 0.0 collective-permute-done.4
  75.0 6.0 %collective-permute-done.5 = bf16[128,256]{1,0:T(8,128)(2,1)S(1)} collective-permute-done((bf16[128,256]{1,0:T(8,128)(2,1)S(1)}, bf16[128,256]{1,0:T(8,128)(2,1)S(1)}, u32[]{:S(2)}, u32[]{:S(2)}) %collective-permute-start.5) | collective-permute-done | bytes 65568 | tf_op jit(solution)/shard_map/ppermute | solution.py:24
  81.0 2.0 %gather_fusion.1 = f32[16,128,256]{2,1,0:T(8,128)} fusion(f32[4,128,256]{2,1,0:T(8,128)S(1)} %convert.8, s32[1024]{0:T(1024)S(1)} %pad_clamp_fusion), kind=kCustom, calls=%fused_computation.1.clone | custom fusion | bytes 4194368 | tf_op jit(solution)/shard_map/jit(_take)/gather | solution.py:58
  83.1 5.4 %bitcast_reduce_fusion.1 = f32[8,128,256]{1,2,0:T(8,128)S(1)} fusion(f32[16,128,128]{2,1,0:T(8,128)S(1)} %copy-done, f32[16,128,256]{2,1,0:T(8,128)} %gather_fusion.1, pred[16]{0:T(512)(128)(4,1)S(1)} %compare_and_fusion), kind=kOutput, calls=%fused_computation.4 | convolution fusion | flops 806092800 | bytes 4194320 | tf_op jit(solution)/shard_map/bij,bjw->biw/dot_general | solution.py:59
  88.5 1.3 copy.17
  89.9 0.0 reduce-scatter.6.cloned.1.call-update
  89.9 0.0 reduce-scatter.8.cloned.1.call-start
  89.9 33.3 %reduce-scatter.6.cloned.1.call-done = f32[128,256]{1,0:T(8,128)} async-done(((f32[1024,256]{1,0:T(8,128)}), f32[128,256]{1,0:T(8,128)}) %reduce-scatter.6.cloned.1.call-update) | async-done | bytes 131088 | tf_op jit(solution)/shard_map/reduce_scatter | solution.py:60
  123.3 1.0 multiply_reduce_fusion.1
  124.3 1.0 constant_dynamic-update-slice_fusion.3
  125.3 1.5 collective-permute-start.6
  126.8 2.3 %collective-permute-start.7 = (bf16[128,256]{1,0:T(8,128)(2,1)S(1)}, bf16[128,256]{1,0:T(8,128)(2,1)S(1)}, u32[]{:S(2)}, u32[]{:S(2)}) collective-permute-start(bf16[128,256]{1,0:T(8,128)(2,1)S(1)} %get-tuple-element.4), channel_id=1, source_target_pairs={{0,3},{1,0},{2,1},{3,2},{4,7},{5,4},{6,5},{7,6},{8,11},{9,8},{10,9... | collective-permute-start | bytes 196616 | tf_op jit(solution)/shard_map/ppermute | solution.py:32
  129.2 2.8 %collective-permute-done.6 = bf16[128,256]{1,0:T(8,128)(2,1)S(1)} collective-permute-done((bf16[128,256]{1,0:T(8,128)(2,1)S(1)}, bf16[128,256]{1,0:T(8,128)(2,1)S(1)}, u32[]{:S(2)}, u32[]{:S(2)}) %collective-permute-start.6) | collective-permute-done | bytes 65568 | tf_op jit(solution)/shard_map/ppermute | solution.py:24
  132.0 0.0 collective-permute-start.8
  132.0 0.0 collective-permute-done.7
  132.0 6.0 %collective-permute-done.8 = bf16[128,256]{1,0:T(8,128)(2,1)S(1)} collective-permute-done((bf16[128,256]{1,0:T(8,128)(2,1)S(1)}, bf16[128,256]{1,0:T(8,128)(2,1)S(1)}, u32[]{:S(2)}, u32[]{:S(2)}) %collective-permute-start.8) | collective-permute-done | bytes 65568 | tf_op jit(solution)/shard_map/ppermute | solution.py:24
  138.1 2.0 %gather_fusion.2 = f32[16,128,256]{2,1,0:T(8,128)} fusion(f32[4,128,256]{2,1,0:T(8,128)S(1)} %convert.10, s32[1024]{0:T(1024)S(1)} %pad_clamp_fusion), kind=kCustom, calls=%fused_computation.2.clone | custom fusion | bytes 4194368 | tf_op jit(solution)/shard_map/jit(_take)/gather | solution.py:58
  140.1 5.4 %bitcast_reduce_fusion = f32[8,128,256]{1,2,0:T(8,128)S(1)} fusion(f32[16,128,128]{2,1,0:T(8,128)S(1)} %copy-done, f32[16,128,256]{2,1,0:T(8,128)} %gather_fusion.2, pred[16]{0:T(512)(128)(4,1)S(1)} %compare_and_fusion), kind=kOutput, calls=%fused_computation.3 | convolution fusion | flops 806092800 | bytes 4194320 | tf_op jit(solution)/shard_map/bij,bjw->biw/dot_general | solution.py:59
  145.6 1.3 copy.19
  146.9 0.0 reduce-scatter.8.cloned.1.call-update
  146.9 33.3 %reduce-scatter.8.cloned.1.call-done = f32[128,256]{1,0:T(8,128)} async-done(((f32[1024,256]{1,0:T(8,128)}), f32[128,256]{1,0:T(8,128)}) %reduce-scatter.8.cloned.1.call-update) | async-done | bytes 131088 | tf_op jit(solution)/shard_map/reduce_scatter | solution.py:60
  180.2 1.0 multiply_reduce_fusion
  181.3 1.0 fusion.19
  182.3 0.7 pad_maximum_fusion
  (27 shorter events, 0.3 us)
Async XLA Ops:
  7.2 17.4 %copy-start = (f32[16,128,128]{2,1,0:T(8,128)S(1)}, f32[16,128,128]{2,1,0:T(8,128)}, u32[]{:S(2)}) copy-start(f32[16,128,128]{2,1,0:T(8,128)} %param.11) | copy-start | bytes 3145732
  7.2 7.0 %copy-start.3 = (s32[16]{0:T(128)S(1)}, s32[16]{0:T(128)}, u32[]{:S(2)}) copy-start(s32[16]{0:T(128)} %param.12) | copy-start | bytes 196
  7.2 59.0 %reduce-scatter.4.cloned.1.call-start = ((), (), s32[]{:S(2)}) async-start(), calls=%async_computation.3 | async-start | bytes 1179648 | tf_op jit(solution)/shard_map/reduce_scatter | solution.py:60
  8.9 15.6 %copy-start.2 = (bf16[128,256]{1,0:T(8,128)(2,1)}, bf16[128,256]{1,0:T(8,128)(2,1)S(1)}, u32[]{:S(2)}) copy-start(bf16[128,256]{1,0:T(8,128)(2,1)S(1)} %get-tuple-element.8) | copy-start | bytes 196612
  9.0 7.5 %collective-permute-start = (bf16[128,256]{1,0:T(8,128)(2,1)S(1)}, bf16[128,256]{1,0:T(8,128)(2,1)S(1)}, u32[]{:S(2)}, u32[]{:S(2)}) collective-permute-start(bf16[128,256]{1,0:T(8,128)(2,1)S(1)} %get-tuple-element.8), channel_id=1, source_target_pairs={{0,1},{1,2},{2,3},{3,0},{4,5},{5,6},{6,7},{7,4},{8,9},{9,10},{10,1... | collective-permute-start | bytes 196616 | tf_op jit(solution)/shard_map/ppermute | solution.py:24
  12.1 5.0 %collective-permute-start.1 = (bf16[128,256]{1,0:T(8,128)(2,1)S(1)}, bf16[128,256]{1,0:T(8,128)(2,1)S(1)}, u32[]{:S(2)}, u32[]{:S(2)}) collective-permute-start(bf16[128,256]{1,0:T(8,128)(2,1)S(1)} %get-tuple-element.8), channel_id=1, source_target_pairs={{0,3},{1,0},{2,1},{3,2},{4,7},{5,4},{6,5},{7,6},{8,11},{9,8},{10,9... | collective-permute-start | bytes 196616 | tf_op jit(solution)/shard_map/ppermute | solution.py:32
  16.4 6.1 %collective-permute-start.2 = (bf16[128,256]{1,0:T(8,128)(2,1)S(1)}, bf16[128,256]{1,0:T(8,128)(2,1)S(1)}, u32[]{:S(2)}, u32[]{:S(2)}) collective-permute-start(bf16[128,256]{1,0:T(8,128)(2,1)S(1)} %collective-permute-done), channel_id=1, source_target_pairs={{0,1},{1,2},{2,3},{3,0},{4,5},{5,6},{6,7},{7,4},{8,9},{9,10},{10,1... | collective-permute-start | bytes 196616 | tf_op jit(solution)/shard_map/ppermute | solution.py:24
  30.0 36.1 %copy-start.1 = (bf16[3,128,256]{2,1,0:T(8,128)(2,1)S(1)}, bf16[3,128,256]{2,1,0:T(8,128)(2,1)}, u32[]{:S(2)}) copy-start(bf16[3,128,256]{2,1,0:T(8,128)(2,1)} %param.13) | copy-start | bytes 589828
  31.4 91.8 %reduce-scatter.6.cloned.1.call-start = ((), (), s32[]{:S(2)}) async-start(), calls=%async_computation.4 | async-start | bytes 1179648 | tf_op jit(solution)/shard_map/reduce_scatter | solution.py:60
  68.2 6.7 %collective-permute-start.3 = (bf16[128,256]{1,0:T(8,128)(2,1)S(1)}, bf16[128,256]{1,0:T(8,128)(2,1)S(1)}, u32[]{:S(2)}, u32[]{:S(2)}) collective-permute-start(bf16[128,256]{1,0:T(8,128)(2,1)S(1)} %get-tuple-element.6), channel_id=1, source_target_pairs={{0,1},{1,2},{2,3},{3,0},{4,5},{5,6},{6,7},{7,4},{8,9},{9,10},{10,1... | collective-permute-start | bytes 196616 | tf_op jit(solution)/shard_map/ppermute | solution.py:24
  69.8 5.2 %collective-permute-start.4 = (bf16[128,256]{1,0:T(8,128)(2,1)S(1)}, bf16[128,256]{1,0:T(8,128)(2,1)S(1)}, u32[]{:S(2)}, u32[]{:S(2)}) collective-permute-start(bf16[128,256]{1,0:T(8,128)(2,1)S(1)} %get-tuple-element.6), channel_id=1, source_target_pairs={{0,3},{1,0},{2,1},{3,2},{4,7},{5,4},{6,5},{7,6},{8,11},{9,8},{10,9... | collective-permute-start | bytes 196616 | tf_op jit(solution)/shard_map/ppermute | solution.py:32
  74.9 6.1 %collective-permute-start.5 = (bf16[128,256]{1,0:T(8,128)(2,1)S(1)}, bf16[128,256]{1,0:T(8,128)(2,1)S(1)}, u32[]{:S(2)}, u32[]{:S(2)}) collective-permute-start(bf16[128,256]{1,0:T(8,128)(2,1)S(1)} %collective-permute-done.3), channel_id=1, source_target_pairs={{0,1},{1,2},{2,3},{3,0},{4,5},{5,6},{6,7},{7,4},{8,9},{9,10},{10,1... | collective-permute-start | bytes 196616 | tf_op jit(solution)/shard_map/ppermute | solution.py:24
  89.9 90.4 %reduce-scatter.8.cloned.1.call-start = ((), (), s32[]{:S(2)}) async-start(), calls=%async_computation.5 | async-start | bytes 1179648 | tf_op jit(solution)/shard_map/reduce_scatter | solution.py:60
  125.3 6.7 %collective-permute-start.6 = (bf16[128,256]{1,0:T(8,128)(2,1)S(1)}, bf16[128,256]{1,0:T(8,128)(2,1)S(1)}, u32[]{:S(2)}, u32[]{:S(2)}) collective-permute-start(bf16[128,256]{1,0:T(8,128)(2,1)S(1)} %get-tuple-element.4), channel_id=1, source_target_pairs={{0,1},{1,2},{2,3},{3,0},{4,5},{5,6},{6,7},{7,4},{8,9},{9,10},{10,1... | collective-permute-start | bytes 196616 | tf_op jit(solution)/shard_map/ppermute | solution.py:24
  126.8 5.1 %collective-permute-start.7 = (bf16[128,256]{1,0:T(8,128)(2,1)S(1)}, bf16[128,256]{1,0:T(8,128)(2,1)S(1)}, u32[]{:S(2)}, u32[]{:S(2)}) collective-permute-start(bf16[128,256]{1,0:T(8,128)(2,1)S(1)} %get-tuple-element.4), channel_id=1, source_target_pairs={{0,3},{1,0},{2,1},{3,2},{4,7},{5,4},{6,5},{7,6},{8,11},{9,8},{10,9... | collective-permute-start | bytes 196616 | tf_op jit(solution)/shard_map/ppermute | solution.py:32
  132.0 6.1 %collective-permute-start.8 = (bf16[128,256]{1,0:T(8,128)(2,1)S(1)}, bf16[128,256]{1,0:T(8,128)(2,1)S(1)}, u32[]{:S(2)}, u32[]{:S(2)}) collective-permute-start(bf16[128,256]{1,0:T(8,128)(2,1)S(1)} %collective-permute-done.6), channel_id=1, source_target_pairs={{0,1},{1,2},{2,3},{3,0},{4,5},{5,6},{6,7},{7,4},{8,9},{9,10},{10,1... | collective-permute-start | bytes 196616 | tf_op jit(solution)/shard_map/ppermute | solution.py:24
Sparse Core Ops, SparseCore 0:
  31.5 34.6 reduce-scatter.3
  90.0 33.2 reduce-scatter.5
  147.0 33.1 reduce-scatter.7
